TPU v7x, 128 devices: a whole 4x4x4 slice. The times are simulated.
128 devices in a mesh: prow: 32 (over x, z_lo, y), pcol: 4 (over z_hi, core).
Axes of the slice: x: 4, y: 4, z: 4 (z_hi: 2, z_lo: 2; z = z_hi * 2 + z_lo), core: 2. Of those that a mesh axis runs over, the one named last changes fastest.
Arguments:
- inverse_band: float32 [4096, 4096], P('prow', 'pcol'), may hold values from -0.09375 to 0.09375
- factor_panel: float32 [2, 4096, 512], P(None, 'prow', 'pcol'), may hold values from -0.6 to 0.6
- diag_inverse: float32 [2, 512, 512], replicated, may hold values from -1 to 2, as said below
- ancestors: int32 [2, 63], replicated, may hold values from 0 to 63, as said below
- counts: int32 [2], replicated, may hold values from 1 to 63, as said below
Outputs:
- new_column: float32 [2, 4096, 512], P(None, 'prow', 'pcol')
- diag_block: float32 [2, 512, 512], P(None, 'prow', 'pcol')
Inputs may be any that keep to these rules, and one draw needn't show every extreme that they name: Each row holds distinct block numbers; its first counts[s] entries are in increasing order and include 63; the entries after them are other block numbers, which are not ancestors. One of the two counts is 63; the other is below 63. `diag_inverse`: lower triangular; diagonal entries from 0.5 to 2.
All inputs are finite; a program needn't handle non-finite values.
Results may differ from a plain program's by a relative error of at most 0.000073.
Values sent between devices are 32-bit elements; how exact they have to be, the bound alone decides.
No kernel may reach another device: no remote copies, remote signals or barrier semaphores. Data moves between devices by JAX's collectives and lax.ppermute only.
A program may use at most 64 MiB of HBM per device.

v0:
```python
import jax
import jax.numpy as jnp
from jax import lax
from jax.sharding import PartitionSpec as P

W = 512
BS = 64
precise = lax.Precision.HIGHEST


def local(inverse_band, factor_panel, diag_inverse, ancestors, counts):
    row_index = lax.axis_index("prow")
    col_index = lax.axis_index("pcol")
    row_devices = lax.axis_size("prow")
    col_devices = lax.axis_size("pcol")
    supernodes = factor_panel.shape[0]
    band_rows = factor_panel.shape[1]
    blocks = band_rows // BS
    quarter = W // col_devices
    block_ids = jnp.arange(blocks, dtype=jnp.int32) * row_devices + row_index
    filled = jnp.arange(ancestors.shape[1], dtype=jnp.int32)[None, :] < counts[:, None]
    matches = (ancestors[:, :, None] == block_ids[None, None, :]) & filled[:, :, None]
    members = jnp.any(matches, axis=1).astype(jnp.float32)
    row_mask = jnp.repeat(members, BS, axis=1)[:, :, None]
    full_panel = lax.all_gather(factor_panel, "pcol", axis=2, tiled=True)
    scaled_panel = (
        jnp.einsum("srk,skw->srw", full_panel, diag_inverse, precision=precise) * row_mask
    )
    own_part = lax.dynamic_slice_in_dim(scaled_panel, col_index * quarter, quarter, 2)
    collected = lax.all_gather(own_part, "prow", axis=1, tiled=True)
    grouped = collected.reshape(
        supernodes, row_devices // col_devices, col_devices, band_rows, quarter
    )
    incoming = lax.all_to_all(grouped, "pcol", split_axis=2, concat_axis=4, tiled=True)
    stacked = incoming.reshape(incoming.shape[0], -1, incoming.shape[-1])
    partial_sums = jnp.einsum("rc,scw->srw", inverse_band, stacked, precision=precise)
    summed = lax.psum_scatter(partial_sums, "pcol", scatter_dimension=2, tiled=True)
    applied = summed * row_mask
    new_column = -applied
    diag_rows = W // row_devices
    product = jnp.einsum("src,srw->csw", scaled_panel, applied, precision=precise)
    reduced = lax.psum_scatter(
        product.reshape(lax.axis_size("prow") * diag_rows, -1),
        "prow",
        scatter_dimension=0,
        tiled=True,
    )
    reduced = reduced.reshape(diag_rows, supernodes, quarter).transpose(1, 0, 2)
    row_factor = lax.dynamic_slice_in_dim(diag_inverse, row_index * diag_rows, diag_rows, 2)
    col_factor = lax.dynamic_slice_in_dim(diag_inverse, col_index * quarter, quarter, 2)
    diag_block = jnp.einsum("skr,skw->srw", row_factor, col_factor, precision=precise) + reduced
    return (new_column, diag_block)


def solution(mesh):
    in_specs = (P("prow", "pcol"), P(None, "prow", "pcol"), P(), P(), P())
    out_specs = (P(None, "prow", "pcol"), P(None, "prow", "pcol"))
    return jax.shard_map(local, mesh=mesh, in_specs=in_specs, out_specs=out_specs, check_vma=False)
```

profile of v0, /device:TPU:0, one launch (start us, length us, event | category | flops | bytes accessed | tf_op | source)
XLA Modules:
  0.0 451.2 jit_solution(8875050085147239257)
XLA Ops:
  7.2 0.0 copy-start
  7.2 0.0 all-gather.2.cloned.1.call-start
  7.2 0.9 iota_compare_fusion
  8.1 0.9 and_reduce_fusion
  9.0 0.1 broadcast_in_dim.2
  9.1 0.1 mul.33
  9.1 9.9 %all_gather.6 = f32[2,128,512]{2,1,0:T(8,128)S(1)} all-gather(f32[2,128,128]{2,1,0:T(8,128)} %param.6), channel_id=1, replica_groups=mesh['prow'=32,'pcol'=4] {'pcol'}, dimensions={2}, use_global_device_ids=true | all-gather | bytes 655360 | tf_op jit(solution)/shard_map/all_gather | solution.py:25
  19.0 0.0 copy-done
  19.0 1.3 convolution_multiply_fusion
  20.3 0.7 constant_dynamic-slice_fusion
  21.0 0.0 all-gather.2.cloned.1.call-update
  21.0 0.0 reduce-scatter.3.cloned.1.call-start
  21.1 157.6 %all-gather.2.cloned.1.call-done = f32[2,4096,128]{2,1,0:T(8,128)} async-done(((f32[2,128,128]{2,1,0:T(8,128)}), f32[2,4096,128]{2,1,0:T(8,128)}) %all-gather.2.cloned.1.call-update) | async-done | bytes 4194320 | tf_op jit(solution)/shard_map/all_gather | solution.py:30
  178.7 2.5 copy.21
  181.1 53.7 %all_to_all.15 = f32[2,8,4,128,128]{4,3,1,0,2:T(8,128)} all-to-all(f32[2,8,4,128,128]{4,3,1,0,2:T(8,128)S(1)} %copy.21), channel_id=1, replica_groups=mesh['prow'=32,'pcol'=4] {'pcol'}, dimensions={2} | all-to-all | bytes 8388608 | tf_op jit(solution)/shard_map/all_to_all | solution.py:34
  234.9 5.2 %copy.22 = f32[2,8,1,128,4,128]{3,1,5,4,0,2:T(8,128)} copy(f32[2,8,1,128,4,128]{5,3,1,0,4,2:T(8,128)} %bitcast.31) | data formatting | bytes 8388608 | tf_op jit(solution)/shard_map/all_to_all | solution.py:34
  240.1 0.0 copy-start.1
  240.1 5.0 %reshape.46 = f32[2,1024,512]{1,2,0:T(8,128)} reshape(f32[2,8,1,128,4,128]{3,1,5,4,0,2:T(8,128)} %copy.22) | data formatting | bytes 8388608 | tf_op jit(solution)/shard_map/reshape | solution.py:35
  245.1 0.0 copy-done.1
  245.1 6.4 %convolution_bitcast_fusion = f32[2,128,512]{1,2,0:T(8,128)} fusion(f32[2,1024,512]{1,2,0:T(8,128)} %reshape.46, f32[128,1024]{1,0:T(8,128)S(1)} %copy-done.1), kind=kOutput, calls=%fused_computation | convolution fusion | flops 1610612736 | bytes 5242880 | tf_op jit(solution)/shard_map/rc,scw->srw/dot_general | solution.py:36
  251.5 0.0 reduce-scatter.3.cloned.1.call-update
  251.5 0.0 reduce-scatter.5.cloned.1.call-start
  251.6 27.0 %reduce-scatter.3.cloned.1.call-done = f32[2,128,128]{1,2,0:T(8,128)} async-done(((f32[2,128,512]{1,2,0:T(8,128)}), f32[2,128,128]{1,2,0:T(8,128)}) %reduce-scatter.3.cloned.1.call-update) | async-done | bytes 131088 | tf_op jit(solution)/shard_map/reduce_scatter | solution.py:37
  278.5 1.5 fusion.3
  280.0 1.0 copy.24
  281.0 0.0 reduce-scatter.5.cloned.1.call-update
  281.0 0.9 multiply_negate_fusion
  282.0 0.8 copy.26
  282.7 159.5 %reduce-scatter.5.cloned.1.call-done = f32[16,256]{1,0:T(8,128)} async-done(((f32[512,256]{1,0:T(8,128)}), f32[16,256]{1,0:T(8,128)}) %reduce-scatter.5.cloned.1.call-update) | async-done | bytes 16400 | tf_op jit(solution)/shard_map/reduce_scatter | solution.py:42
  442.2 2.5 convolution_add_fusion
  (2 shorter events, 0.0 us)
Async XLA Ops:
  7.2 11.8 %copy-start = (f32[2,512,512]{2,1,0:T(8,128)S(1)}, f32[2,512,512]{2,1,0:T(8,128)}, u32[]{:S(2)}) copy-start(f32[2,512,512]{2,1,0:T(8,128)} %param.7) | copy-start | bytes 6291460
  7.2 171.5 %all-gather.2.cloned.1.call-start = ((), (), s32[]{:S(2)}) async-start(), calls=%async_computation.3 | async-start | bytes 4325376 | tf_op jit(solution)/shard_map/all_gather | solution.py:30
  21.0 257.5 %reduce-scatter.3.cloned.1.call-start = ((), (), s32[]{:S(2)}) async-start(), calls=%async_computation.4 | async-start | bytes 655360 | tf_op jit(solution)/shard_map/reduce_scatter | solution.py:37
  240.1 5.0 %copy-start.1 = (f32[128,1024]{1,0:T(8,128)S(1)}, f32[128,1024]{1,0:T(8,128)}, u32[]{:S(2)}) copy-start(f32[128,1024]{1,0:T(8,128)} %param.5) | copy-start | bytes 1572868
  251.5 190.7 %reduce-scatter.5.cloned.1.call-start = ((), (), s32[]{:S(2)}) async-start(), calls=%async_computation.5 | async-start | bytes 540672 | tf_op jit(solution)/shard_map/reduce_scatter | solution.py:42
Sparse Core Ops, SparseCore 0:
  21.1 157.5 all-gather.1
  251.6 26.8 reduce-scatter.2
  281.2 161.0 reduce-scatter.4
where the time goes:
time: 452 us; the launch traced here: 451 us
  waiting for transfers between devices  344 us (76%)
  blocking collectives  63.6 us (14%)
  local copies, waits for them, and re-layouts  15.3 us (3%)
  between operations  13.8 us (3%)
  matrix products  11.7 us (3%)
    reduce_scatter x1, waiting for transfers between devices, local(): lax.psum_scatter(product.reshape(lax.axis_size('prow') * diag_rows, -1),...  159 us
    all_gather x1, waiting for transfers between devices, local(): collected = lax.all_gather(own_part, 'prow', axis=1, tiled=True)  158 us
    all_to_all x1, blocking collectives, local(): lax.all_to_all(grouped, 'pcol', split_axis=2, concat_axis=4, tiled=True)  53.7 us
    reduce_scatter x1, waiting for transfers between devices, local(): lax.psum_scatter(partial_sums, 'pcol', scatter_dimension=2, tiled=True)  27 us
    all_gather x1, blocking collectives, local(): full_panel = lax.all_gather(factor_panel, 'pcol', axis=2, tiled=True)  9.87 us
  transfers between devices with their start and end apart: 3, of which 3 were waited for; matrix products, arithmetic and copies ran while one was open for 0% of the time, Pallas kernels for 0%

commit v1 on v0

--- a/solution.py
+++ b/solution.py
@@ -27,7 +27,9 @@
         jnp.einsum("srk,skw->srw", full_panel, diag_inverse, precision=precise) * row_mask
     )
     own_part = lax.dynamic_slice_in_dim(scaled_panel, col_index * quarter, quarter, 2)
-    collected = lax.all_gather(own_part, "prow", axis=1, tiled=True)
+    collected = jnp.concatenate(
+        lax.all_to_all(jnp.stack([own_part] * lax.axis_size("prow")), "prow", 0, 0), axis=1
+    )
     grouped = collected.reshape(
         supernodes, row_devices // col_devices, col_devices, band_rows, quarter
     )

time: 452 us -> 350 us (0.77)
  waiting for transfers between devices: 344 us -> 186 us
  blocking collectives: 63.6 us -> 122 us
    all_gather x1 -> x0, waiting for transfers between devices: 158 us -> none  [local(): collected = lax.all_gather(own_part, 'prow', axis=1, tiled=True)]
    all_to_all x0 -> x1, blocking collectives: none -> 58.2 us  [local(): lax.all_to_all(jnp.stack([own_part] * lax.axis_size('prow')), 'prow', 0, 0)]
  transfers between devices with their start and end apart: 3 -> 2, of which waited for: 3 -> 2; matrix products, arithmetic and copies ran while one was open for 0% -> 0% of each run, Pallas kernels for 0% -> 0%
where the time goes in v1:
time: 350 us
  waiting for transfers between devices  186 us (53%)
  blocking collectives  122 us (35%)
  between operations  14.1 us (4%)
  local copies, waits for them, and re-layouts  13.1 us (4%)
  matrix products  11.7 us (3%)
    reduce_scatter x1, waiting for transfers between devices, local(): lax.psum_scatter(product.reshape(lax.axis_size('prow') * diag_rows, -1),...  160 us
    all_to_all x1, blocking collectives, local(): lax.all_to_all(jnp.stack([own_part] * lax.axis_size('prow')), 'prow', 0, 0)  58.2 us
    all_to_all x1, blocking collectives, local(): lax.all_to_all(grouped, 'pcol', split_axis=2, concat_axis=4, tiled=True)  54 us
    reduce_scatter x1, waiting for transfers between devices, local(): lax.psum_scatter(partial_sums, 'pcol', scatter_dimension=2, tiled=True)  26.1 us
    all_gather x1, blocking collectives, local(): full_panel = lax.all_gather(factor_panel, 'pcol', axis=2, tiled=True)  9.87 us
  transfers between devices with their start and end apart: 2, of which 2 were waited for; matrix products, arithmetic and copies ran while one was open for 0% of the time, Pallas kernels for 0%

profile of v1, /device:TPU:0, one launch (start us, length us, event | category | flops | bytes accessed | tf_op | source)
XLA Modules:
  0.0 349.7 jit_solution(1106226784478211457)
XLA Ops:
  7.2 0.0 copy-start
  7.2 0.0 reduce-scatter.3.cloned.1.call-start
  7.2 0.9 iota_compare_fusion
  8.1 0.9 and_reduce_fusion
  9.0 0.1 broadcast_in_dim.2
  9.1 0.1 mul.33
  9.1 9.9 %all_gather.3 = f32[2,128,512]{2,1,0:T(8,128)S(1)} all-gather(f32[2,128,128]{2,1,0:T(8,128)} %param.6), channel_id=1, replica_groups=mesh['prow'=32,'pcol'=4] {'pcol'}, dimensions={2}, use_global_device_ids=true | all-gather | bytes 655360 | tf_op jit(solution)/shard_map/all_gather | solution.py:25
  19.0 0.0 copy-done
  19.0 1.3 convolution_multiply_fusion
  20.3 0.5 stack.2
  20.8 58.2 %all_to_all.20 = f32[32,2,128,128]{3,2,1,0:T(8,128)S(1)} all-to-all(f32[32,2,128,128]{3,2,1,0:T(8,128)S(1)} %stack.2), channel_id=1, replica_groups=mesh['prow'=32,'pcol'=4] {'prow'}, dimensions={0} | all-to-all | bytes 8388608 | tf_op jit(solution)/shard_map/all_to_all | solution.py:31
  79.0 0.5 copy.22
  79.5 54.0 %all_to_all.21 = f32[2,8,4,128,128]{4,3,1,0,2:T(8,128)} all-to-all(f32[2,8,4,128,128]{4,3,1,0,2:T(8,128)S(1)} %copy.22), channel_id=1, replica_groups=mesh['prow'=32,'pcol'=4] {'pcol'}, dimensions={2} | all-to-all | bytes 8388608 | tf_op jit(solution)/shard_map/all_to_all | solution.py:36
  133.5 5.2 %copy.23 = f32[2,8,1,128,4,128]{3,1,5,4,0,2:T(8,128)} copy(f32[2,8,1,128,4,128]{5,3,1,0,4,2:T(8,128)} %bitcast.34) | data formatting | bytes 8388608 | tf_op jit(solution)/shard_map/all_to_all | solution.py:36
  138.8 0.0 copy-start.1
  138.8 5.0 %reshape.48 = f32[2,1024,512]{1,2,0:T(8,128)} reshape(f32[2,8,1,128,4,128]{3,1,5,4,0,2:T(8,128)} %copy.23) | data formatting | bytes 8388608 | tf_op jit(solution)/shard_map/reshape | solution.py:37
  143.7 0.0 copy-done.1
  143.7 6.4 %convolution_bitcast_fusion = f32[2,128,512]{1,2,0:T(8,128)} fusion(f32[2,1024,512]{1,2,0:T(8,128)} %reshape.48, f32[128,1024]{1,0:T(8,128)S(1)} %copy-done.1), kind=kOutput, calls=%fused_computation | convolution fusion | flops 1610612736 | bytes 5242880 | tf_op jit(solution)/shard_map/rc,scw->srw/dot_general | solution.py:38
  150.1 0.0 reduce-scatter.3.cloned.1.call-update
  150.2 0.0 reduce-scatter.5.cloned.1.call-start
  150.2 26.1 %reduce-scatter.3.cloned.1.call-done = f32[2,128,128]{1,2,0:T(8,128)} async-done(((f32[2,128,512]{1,2,0:T(8,128)}), f32[2,128,128]{1,2,0:T(8,128)}) %reduce-scatter.3.cloned.1.call-update) | async-done | bytes 131088 | tf_op jit(solution)/shard_map/reduce_scatter | solution.py:39
  176.3 1.5 fusion.3
  177.8 1.0 copy.25
  178.8 0.0 reduce-scatter.5.cloned.1.call-update
  178.8 0.9 multiply_negate_fusion
  179.8 0.8 copy.27
  180.5 159.9 %reduce-scatter.5.cloned.1.call-done = f32[16,256]{1,0:T(8,128)} async-done(((f32[512,256]{1,0:T(8,128)}), f32[16,256]{1,0:T(8,128)}) %reduce-scatter.5.cloned.1.call-update) | async-done | bytes 16400 | tf_op jit(solution)/shard_map/reduce_scatter | solution.py:44
  340.4 2.5 convolution_add_fusion
  (3 shorter events, 0.0 us)
Async XLA Ops:
  7.2 11.8 %copy-start = (f32[2,512,512]{2,1,0:T(8,128)S(1)}, f32[2,512,512]{2,1,0:T(8,128)}, u32[]{:S(2)}) copy-start(f32[2,512,512]{2,1,0:T(8,128)} %param.7) | copy-start | bytes 6291460
  7.2 169.1 %reduce-scatter.3.cloned.1.call-start = ((), (), s32[]{:S(2)}) async-start(), calls=%async_computation.4 | async-start | bytes 655360 | tf_op jit(solution)/shard_map/reduce_scatter | solution.py:39
  138.8 5.0 %copy-start.1 = (f32[128,1024]{1,0:T(8,128)S(1)}, f32[128,1024]{1,0:T(8,128)}, u32[]{:S(2)}) copy-start(f32[128,1024]{1,0:T(8,128)} %param.5) | copy-start | bytes 1572868
  150.2 190.2 %reduce-scatter.5.cloned.1.call-start = ((), (), s32[]{:S(2)}) async-start(), calls=%async_computation.5 | async-start | bytes 540672 | tf_op jit(solution)/shard_map/reduce_scatter | solution.py:44
Sparse Core Ops, SparseCore 0:
  150.3 26.0 reduce-scatter.2
  179.0 161.3 reduce-scatter.4
